TPU v7x, 32 devices: a whole 2x2x4 slice. The times are simulated.
32 devices in a mesh: seq: 8 (over y, x, core), slot: 4 (over z).
Axes of the slice: x: 2, y: 2, z: 4, core: 2. Of those that a mesh axis runs over, the one named last changes fastest.
Arguments:
- tokens: bfloat16 [8, 1024, 768], P('slot', 'seq'), may hold values from -6 to 6
- qkv_weight: bfloat16 [768, 2304], P(('seq', 'slot')), may hold values from -0.21875 to 0.21875
- query_bias: bfloat16 [768], P(('seq', 'slot')), may hold values from -3 to 3
- value_bias: bfloat16 [768], P(('seq', 'slot')), may hold values from -3 to 3
- out_weight: bfloat16 [768, 768], P(('seq', 'slot')), may hold values from -6 to 6
- out_bias: bfloat16 [768], P(('seq', 'slot')), may hold values from -3 to 3
- norm1_gain: bfloat16 [768], P(('seq', 'slot')), may hold values from 0.25 to 1.75
- norm1_shift: bfloat16 [768], P(('seq', 'slot')), may hold values from -2 to 2
- up_weight: bfloat16 [768, 3072], P(('seq', 'slot')), may hold values from -0.21875 to 0.21875
- up_bias: bfloat16 [3072], P(('seq', 'slot')), may hold values from -3 to 3
- down_weight: bfloat16 [3072, 768], P(('seq', 'slot')), may hold values from -0.109375 to 0.109375
- down_bias: bfloat16 [768], P(('seq', 'slot')), may hold values from -3 to 3
- norm2_gain: bfloat16 [768], P(('seq', 'slot')), may hold values from 0.25 to 1.75
- norm2_shift: bfloat16 [768], P(('seq', 'slot')), may hold values from -2 to 2
- slot_lengths: int32 [8], P('slot'), may hold values from 256 to 1024, as said below
- out_cotangent: bfloat16 [8, 1024, 768], P('slot', 'seq'), may hold values from -6 to 6
Outputs:
- layer_out: bfloat16 [8, 1024, 768], P('slot', 'seq')
- tokens_grad: bfloat16 [8, 1024, 768], P('slot', 'seq')
- qkv_weight_grad: float32 [768, 2304], P(('seq', 'slot'))
- query_bias_grad: float32 [768], P(('seq', 'slot'))
- value_bias_grad: float32 [768], P(('seq', 'slot'))
- out_weight_grad: float32 [768, 768], P(('seq', 'slot'))
- out_bias_grad: float32 [768], P(('seq', 'slot'))
- norm1_gain_grad: float32 [768], P(('seq', 'slot'))
- norm1_shift_grad: float32 [768], P(('seq', 'slot'))
- up_weight_grad: float32 [768, 3072], P(('seq', 'slot'))
- up_bias_grad: float32 [3072], P(('seq', 'slot'))
- down_weight_grad: float32 [3072, 768], P(('seq', 'slot'))
- down_bias_grad: float32 [768], P(('seq', 'slot'))
- norm2_gain_grad: float32 [768], P(('seq', 'slot'))
- norm2_shift_grad: float32 [768], P(('seq', 'slot'))
Inputs may be any that keep to these rules, and one draw needn't show every extreme that they name: `slot_lengths`: the valid tokens of each slot stand at its start; some slot is full and some holds 256 tokens.
All inputs are finite; a program needn't handle non-finite values.
Results may differ from a plain program's by a relative error of at most 0.015.
Values may be sent and summed in bfloat16 or wider, within the bound.
No kernel may reach another device: no remote copies, remote signals or barrier semaphores. Data moves between devices by JAX's collectives and lax.ppermute only.
A program may use at most 192 MiB of HBM per device.

v0:
```python
import jax
import jax.numpy as jnp
from jax import lax
from jax.sharding import PartitionSpec as P

HEADS = 12
NEG_FILL = -1e30
EPSILON = 1e-05


def norm_rows(resid, gain, shift):
    centre = resid - jnp.mean(resid, -1, keepdims=True)
    spread = jnp.mean(centre * centre, -1, keepdims=True)
    return centre * lax.rsqrt(spread + EPSILON) * gain + shift


def gelu_exact(inner_act):
    return jax.nn.gelu(inner_act, approximate=False)


def contract_rows(left, right):
    return lax.dot_general(
        left, right, (((0,), (0,)), ((), ())), preferred_element_type=jnp.float32
    )


def contract_last(left, right):
    return lax.dot_general(
        left, right, (((1,), (1,)), ((), ())), preferred_element_type=jnp.float32
    )


def split_heads(rows_in, head_count):
    return rows_in.reshape(
        rows_in.shape[0], rows_in.shape[1], head_count, rows_in.shape[2] // head_count
    )


def take_block(whole, position, block_size, axis_dim):
    return lax.dynamic_slice_in_dim(whole, position * block_size, block_size, axis_dim)


def masked_scores(queries, key_rows, key_start, slot_lengths):
    scores = jnp.einsum("sqhd,skhd->shqk", queries, key_rows, preferred_element_type=jnp.float32)
    key_places = key_start + jnp.arange(key_rows.shape[1])
    live_keys = key_places[None, :] < slot_lengths[:, None]
    return jnp.where(live_keys[:, None, None, :], scores, NEG_FILL)


def log_totals(queries, key_all, slot_lengths, block_size, head_count):
    block_count = key_all.shape[1] // block_size
    stat_shape = (queries.shape[0], head_count, queries.shape[1])

    def log_step_fn(carried, position):
        running_max, running_sum = carried
        key_rows = split_heads(take_block(key_all, position, block_size, 1), head_count)
        scores = masked_scores(queries, key_rows, position * block_size, slot_lengths)
        new_max = jnp.maximum(running_max, jnp.max(scores, -1))
        running_sum = running_sum * jnp.exp(running_max - new_max) + jnp.sum(
            jnp.exp(scores - new_max[..., None]), -1
        )
        return ((new_max, running_sum), None)

    start_state = (jnp.full(stat_shape, NEG_FILL, jnp.float32), jnp.zeros(stat_shape, jnp.float32))
    (running_max, running_sum), _ = lax.scan(log_step_fn, start_state, jnp.arange(block_count))
    return running_max + jnp.log(running_sum)


def attend(queries, key_all, value_all, slot_lengths, logsum, block_size, head_count):
    block_count = key_all.shape[1] // block_size

    def attend_step_fn(context, position):
        key_rows = split_heads(take_block(key_all, position, block_size, 1), head_count)
        value_rows = split_heads(take_block(value_all, position, block_size, 1), head_count)
        scores = masked_scores(queries, key_rows, position * block_size, slot_lengths)
        weights_low = jnp.exp(scores - logsum[..., None]).astype(jnp.bfloat16)
        return (
            context
            + jnp.einsum(
                "shqk,skhd->sqhd", weights_low, value_rows, preferred_element_type=jnp.float32
            ),
            None,
        )

    context, _ = lax.scan(
        attend_step_fn, jnp.zeros(queries.shape, jnp.float32), jnp.arange(block_count)
    )
    return context


def prob_grad_totals(
    queries, d_context, key_all, value_all, slot_lengths, logsum, block_size, head_count
):
    block_count = key_all.shape[1] // block_size

    def prob_step_fn(prob_delta, position):
        key_rows = split_heads(take_block(key_all, position, block_size, 1), head_count)
        value_rows = split_heads(take_block(value_all, position, block_size, 1), head_count)
        scores = masked_scores(queries, key_rows, position * block_size, slot_lengths)
        softmax_rows = jnp.exp(scores - logsum[..., None])
        d_probs = jnp.einsum(
            "sqhd,skhd->shqk", d_context, value_rows, preferred_element_type=jnp.float32
        )
        return (prob_delta + jnp.sum(softmax_rows * d_probs, -1), None)

    prob_delta, _ = lax.scan(
        prob_step_fn, jnp.zeros(logsum.shape, jnp.float32), jnp.arange(block_count)
    )
    return prob_delta


def key_side(
    queries, d_context, key_all, value_all, slot_lengths, logsum, prob_delta, block_size, head_count
):
    block_count = key_all.shape[1] // block_size

    def key_step_fn(d_query, position):
        key_rows = split_heads(take_block(key_all, position, block_size, 1), head_count)
        value_rows = split_heads(take_block(value_all, position, block_size, 1), head_count)
        scores = masked_scores(queries, key_rows, position * block_size, slot_lengths)
        softmax_rows = jnp.exp(scores - logsum[..., None])
        d_probs = jnp.einsum(
            "sqhd,skhd->shqk", d_context, value_rows, preferred_element_type=jnp.float32
        )
        d_scores = (softmax_rows * (d_probs - prob_delta[..., None])).astype(jnp.bfloat16)
        d_query = d_query + jnp.einsum(
            "shqk,skhd->sqhd", d_scores, key_rows, preferred_element_type=jnp.float32
        )
        d_key_rows = jnp.einsum(
            "shqk,sqhd->skhd", d_scores, queries, preferred_element_type=jnp.float32
        )
        d_value_rows = jnp.einsum(
            "shqk,sqhd->skhd",
            softmax_rows.astype(jnp.bfloat16),
            d_context,
            preferred_element_type=jnp.float32,
        )
        return (d_query, (d_key_rows, d_value_rows))

    return lax.scan(key_step_fn, jnp.zeros(queries.shape, jnp.float32), jnp.arange(block_count))


def body(
    tokens,
    qkv_weight,
    query_bias,
    value_bias,
    out_weight,
    out_bias,
    norm1_gain,
    norm1_shift,
    up_weight,
    up_bias,
    down_weight,
    down_bias,
    norm2_gain,
    norm2_shift,
    slot_lengths,
    out_cotangent,
):
    slot_count, row_count, model_width = tokens.shape
    head_count = HEADS
    flat_rows = tokens.reshape(slot_count * row_count, model_width)
    attn_set = (
        lax.all_gather(qkv_weight, ("seq", "slot"), axis=0, tiled=True),
        lax.all_gather(out_weight, ("seq", "slot"), axis=0, tiled=True),
        lax.all_gather(query_bias, ("seq", "slot"), axis=0, tiled=True),
        lax.all_gather(value_bias, ("seq", "slot"), axis=0, tiled=True),
        lax.all_gather(out_bias, ("seq", "slot"), axis=0, tiled=True),
        lax.all_gather(norm1_gain, ("seq", "slot"), axis=0, tiled=True),
        lax.all_gather(norm1_shift, ("seq", "slot"), axis=0, tiled=True),
    )
    qkv_full, out_full, query_shift, value_shift, out_shift, gain_one, shift_one = attn_set
    mixed = jnp.dot(flat_rows, qkv_full, preferred_element_type=jnp.float32)
    queries = ((mixed[:, :model_width] + query_shift.astype(jnp.float32)) * 0.125).astype(
        jnp.bfloat16
    )
    queries = split_heads(queries.reshape(slot_count, row_count, model_width), head_count)
    keys_own = (
        mixed[:, model_width : 2 * model_width]
        .astype(jnp.bfloat16)
        .reshape(slot_count, row_count, model_width)
    )
    values_own = (
        (mixed[:, 2 * model_width :] + value_shift.astype(jnp.float32))
        .astype(jnp.bfloat16)
        .reshape(slot_count, row_count, model_width)
    )
    key_all, value_all = (
        lax.all_gather(keys_own, "seq", axis=1, tiled=True),
        lax.all_gather(values_own, "seq", axis=1, tiled=True),
    )
    length_all = key_all.shape[1]
    block_size = min(512, length_all)
    logsum = log_totals(queries, key_all, slot_lengths, block_size, head_count)
    context = attend(
        queries, key_all, value_all, slot_lengths, logsum, block_size, head_count
    ).astype(jnp.bfloat16)
    context_flat = context.reshape(slot_count * row_count, model_width)
    attn_out = jnp.dot(
        context_flat, out_full, preferred_element_type=jnp.float32
    ) + out_shift.astype(jnp.float32)
    resid_one = flat_rows.astype(jnp.float32) + attn_out
    hidden_one = norm_rows(resid_one, gain_one.astype(jnp.float32), shift_one.astype(jnp.float32))
    hidden_low = hidden_one.astype(jnp.bfloat16)
    ffn_set = (
        lax.all_gather(up_weight, ("seq", "slot"), axis=0, tiled=True),
        lax.all_gather(down_weight, ("seq", "slot"), axis=0, tiled=True),
        lax.all_gather(up_bias, ("seq", "slot"), axis=0, tiled=True),
        lax.all_gather(down_bias, ("seq", "slot"), axis=0, tiled=True),
        lax.all_gather(norm2_gain, ("seq", "slot"), axis=0, tiled=True),
        lax.all_gather(norm2_shift, ("seq", "slot"), axis=0, tiled=True),
    )
    up_full, down_full, up_shift, down_shift, gain_two, shift_two = ffn_set
    inner_act = jnp.dot(hidden_low, up_full, preferred_element_type=jnp.float32) + up_shift.astype(
        jnp.float32
    )
    activated = gelu_exact(inner_act).astype(jnp.bfloat16)
    ffn_out = jnp.dot(activated, down_full, preferred_element_type=jnp.float32) + down_shift.astype(
        jnp.float32
    )
    resid_two = hidden_one + ffn_out
    layer_out = norm_rows(resid_two, gain_two.astype(jnp.float32), shift_two.astype(jnp.float32))
    layer_out = layer_out.astype(jnp.bfloat16).reshape(slot_count, row_count, model_width)
    qkv_back, out_back, _, _, _, gain_one_back, shift_one_back = (
        lax.all_gather(qkv_weight, ("seq", "slot"), axis=0, tiled=True),
        lax.all_gather(out_weight, ("seq", "slot"), axis=0, tiled=True),
        lax.all_gather(query_bias, ("seq", "slot"), axis=0, tiled=True),
        lax.all_gather(value_bias, ("seq", "slot"), axis=0, tiled=True),
        lax.all_gather(out_bias, ("seq", "slot"), axis=0, tiled=True),
        lax.all_gather(norm1_gain, ("seq", "slot"), axis=0, tiled=True),
        lax.all_gather(norm1_shift, ("seq", "slot"), axis=0, tiled=True),
    )
    up_back, down_back, _, _, gain_two_back, shift_two_back = (
        lax.all_gather(up_weight, ("seq", "slot"), axis=0, tiled=True),
        lax.all_gather(down_weight, ("seq", "slot"), axis=0, tiled=True),
        lax.all_gather(up_bias, ("seq", "slot"), axis=0, tiled=True),
        lax.all_gather(down_bias, ("seq", "slot"), axis=0, tiled=True),
        lax.all_gather(norm2_gain, ("seq", "slot"), axis=0, tiled=True),
        lax.all_gather(norm2_shift, ("seq", "slot"), axis=0, tiled=True),
    )
    positions = lax.axis_index("seq") * row_count + jnp.arange(row_count)
    live_rows = (positions[None, :] < slot_lengths[:, None]).astype(jnp.float32)
    cotangent = (out_cotangent.astype(jnp.float32) * live_rows[:, :, None]).reshape(
        slot_count * row_count, model_width
    )
    _, norm_back_two = jax.vjp(
        norm_rows, resid_two, gain_two_back.astype(jnp.float32), shift_two_back.astype(jnp.float32)
    )
    d_resid_two, d_gain_two, d_shift_two = norm_back_two(cotangent)
    d_ffn = d_resid_two.astype(jnp.bfloat16)
    d_down = contract_rows(activated, d_ffn)
    d_down_shift = jnp.sum(d_ffn.astype(jnp.float32), 0)
    d_activated = contract_last(d_ffn, down_back)
    _, gelu_back = jax.vjp(gelu_exact, inner_act)
    d_inner = gelu_back(d_activated)[0].astype(jnp.bfloat16)
    d_up = contract_rows(hidden_low, d_inner)
    d_up_shift = jnp.sum(d_inner.astype(jnp.float32), 0)
    d_hidden = contract_last(d_inner, up_back) + d_resid_two
    _, norm_back_one = jax.vjp(
        norm_rows, resid_one, gain_one_back.astype(jnp.float32), shift_one_back.astype(jnp.float32)
    )
    d_resid_one, d_gain_one, d_shift_one = norm_back_one(d_hidden)
    d_attn = d_resid_one.astype(jnp.bfloat16)
    d_out = contract_rows(context_flat, d_attn)
    d_out_shift = jnp.sum(d_attn.astype(jnp.float32), 0)
    d_context = contract_last(d_attn, out_back).astype(jnp.bfloat16)
    d_context = split_heads(d_context.reshape(slot_count, row_count, model_width), head_count)
    prob_delta = prob_grad_totals(
        queries, d_context, key_all, value_all, slot_lengths, logsum, block_size, head_count
    )
    d_query, key_parts = key_side(
        queries,
        d_context,
        key_all,
        value_all,
        slot_lengths,
        logsum,
        prob_delta,
        block_size,
        head_count,
    )
    d_key_part = jnp.moveaxis(key_parts[0], 0, 1).reshape(slot_count, length_all, model_width)
    d_value_part = jnp.moveaxis(key_parts[1], 0, 1).reshape(slot_count, length_all, model_width)
    d_key_sum, d_value_sum = (
        lax.psum_scatter(
            d_key_part.astype(jnp.bfloat16), "seq", scatter_dimension=1, tiled=True
        ).astype(jnp.float32),
        lax.psum_scatter(
            d_value_part.astype(jnp.bfloat16), "seq", scatter_dimension=1, tiled=True
        ).astype(jnp.float32),
    )
    d_query_pre = d_query.astype(jnp.bfloat16).reshape(
        slot_count * row_count, model_width
    ) * jnp.asarray(0.125, jnp.bfloat16)
    d_key_low = d_key_sum.astype(jnp.bfloat16).reshape(slot_count * row_count, model_width)
    d_value_low = d_value_sum.astype(jnp.bfloat16).reshape(slot_count * row_count, model_width)
    d_mixed = jnp.concatenate([d_query_pre, d_key_low, d_value_low], 1)
    d_qkv = contract_rows(flat_rows, d_mixed)
    d_query_shift = jnp.sum(d_query_pre.astype(jnp.float32), 0)
    d_value_shift = jnp.sum(d_value_low.astype(jnp.float32), 0)
    tokens_grad = (
        (d_resid_one + contract_last(d_mixed, qkv_back))
        .astype(jnp.bfloat16)
        .reshape(slot_count, row_count, model_width)
    )
    attn_sums = (
        lax.psum_scatter(d_qkv, ("seq", "slot"), scatter_dimension=0, tiled=True),
        lax.psum_scatter(d_out, ("seq", "slot"), scatter_dimension=0, tiled=True),
        lax.psum_scatter(d_query_shift, ("seq", "slot"), scatter_dimension=0, tiled=True),
        lax.psum_scatter(d_value_shift, ("seq", "slot"), scatter_dimension=0, tiled=True),
        lax.psum_scatter(d_out_shift, ("seq", "slot"), scatter_dimension=0, tiled=True),
        lax.psum_scatter(d_gain_one, ("seq", "slot"), scatter_dimension=0, tiled=True),
        lax.psum_scatter(d_shift_one, ("seq", "slot"), scatter_dimension=0, tiled=True),
    )
    ffn_sums = (
        lax.psum_scatter(d_up, ("seq", "slot"), scatter_dimension=0, tiled=True),
        lax.psum_scatter(d_down, ("seq", "slot"), scatter_dimension=0, tiled=True),
        lax.psum_scatter(d_up_shift, ("seq", "slot"), scatter_dimension=0, tiled=True),
        lax.psum_scatter(d_down_shift, ("seq", "slot"), scatter_dimension=0, tiled=True),
        lax.psum_scatter(d_gain_two, ("seq", "slot"), scatter_dimension=0, tiled=True),
        lax.psum_scatter(d_shift_two, ("seq", "slot"), scatter_dimension=0, tiled=True),
    )
    return (
        layer_out,
        tokens_grad,
        attn_sums[0],
        attn_sums[2],
        attn_sums[3],
        attn_sums[1],
        attn_sums[4],
        attn_sums[5],
        attn_sums[6],
        ffn_sums[0],
        ffn_sums[2],
        ffn_sums[1],
        ffn_sums[3],
        ffn_sums[4],
        ffn_sums[5],
    )


def solution(mesh):
    return jax.shard_map(
        body,
        mesh=mesh,
        in_specs=(
            P("slot", "seq", None),
            P(("seq", "slot"), None),
            P(("seq", "slot")),
            P(("seq", "slot")),
            P(("seq", "slot"), None),
            P(("seq", "slot")),
            P(("seq", "slot")),
            P(("seq", "slot")),
            P(("seq", "slot"), None),
            P(("seq", "slot")),
            P(("seq", "slot"), None),
            P(("seq", "slot")),
            P(("seq", "slot")),
            P(("seq", "slot")),
            P("slot"),
            P("slot", "seq", None),
        ),
        out_specs=(
            P("slot", "seq", None),
            P("slot", "seq", None),
            P(("seq", "slot"), None),
            P(("seq", "slot")),
            P(("seq", "slot")),
            P(("seq", "slot"), None),
            P(("seq", "slot")),
            P(("seq", "slot")),
            P(("seq", "slot")),
            P(("seq", "slot"), None),
            P(("seq", "slot")),
            P(("seq", "slot"), None),
            P(("seq", "slot")),
            P(("seq", "slot")),
            P(("seq", "slot")),
        ),
        check_vma=False,
    )
```

profile of v0, /device:TPU:0, one launch (start us, length us, event | category | flops | bytes accessed | tf_op | source)
XLA Modules:
  0.0 1040.6 jit_solution(14820919905901474009)
XLA Ops:
  8.0 65.6 %all-gather.7.cloned.1.call-done = bf16[768,2304]{1,0:T(8,128)(2,1)} async-done(((bf16[24,2304]{1,0:T(8,128)(2,1)}), bf16[768,2304]{1,0:T(8,128)(2,1)}) %all-gather.7.cloned.1.call-update) | async-done | bytes 3538960 | tf_op jit(solution)/shard_map/all_gather | solution.py:165
  73.6 3.3 fusion.54
  80.2 39.2 %all-reduce.19 = (bf16[3072]{0:T(1024)(128)(2,1)S(1)}, bf16[768]{0:T(1024)(128)(2,1)}, bf16[768]{0:T(1024)(128)(2,1)S(1)}, bf16[768]{0:T(1024)(128)(2,1)S(1)}, b...) all-reduce(bf16[3072]{0:T(1024)(128)(2,1)S(1)} %dynamic-update-slic, ...), channel_id=1, replica_groups=mesh['seq'=8,'slot'=4] {'seq','slot'}, use_global_device_ids=true, to_apply=%add.5 | all-reduce | flops 9216 | bytes 36864
  132.4 21.4 %while.50 = (s32[]{:T(128)}, f32[2,12,128]{2,1,0:T(8,128)S(1)}, f32[2,12,128]{2,1,0:T(8,128)S(1)}, s32[2]{0:T(128)S(1)}, s32[2]{0:T(128)S(1)}, /*index=5*/bf16[2...) while((s32[]{:T(128)}, f32[2,12,128]{2,1,0:T(8,128)S(1)}, ...), condition=%wide.region_3.4_spmd.clone, body=%wide.region_0.3_spmd.clone.sunk | while | flops 209207808 | bytes 17861824 | solution.py:65
  135.3 4.1 bitcast_reduce_fusion.2
  139.4 3.9 fusion.121
  146.1 4.1 bitcast_reduce_fusion.2
  150.2 3.5 fusion.121
  154.5 17.4 %while.51 = (s32[]{:T(128)}, f32[2,128,12,64]{1,3,2,0:T(8,128)}, s32[2]{0:T(128)}, bf16[2,1024,768]{1,2,0:T(8,128)(2,1)}, s32[2]{0:T(128)}, /*index=5*/bf16[2,10...) while((s32[]{:T(128)}, f32[2,128,12,64]{1,3,2,0:T(8,128)}, ...), condition=%wide.region_5.6_spmd.clone, body=%wide.region_4.5_spmd.clone.sunk | while | flops 407766528 | bytes 11421957 | solution.py:85
  159.1 3.8 fusion.126
  167.6 4.2 fusion.126
  173.5 37.2 %all-gather.13.cloned.1.call-done = bf16[768,768]{1,0:T(8,128)(2,1)} async-done(((bf16[24,768]{1,0:T(8,128)(2,1)}), bf16[768,768]{1,0:T(8,128)(2,1)}) %all-gather.13.cloned.1.call-update) | async-done | bytes 1179664 | tf_op jit(solution)/shard_map/all_gather | solution.py:166
  212.9 62.9 %all-gather.15.cloned.1.call-done = bf16[768,3072]{1,0:T(8,128)(2,1)} async-done(((bf16[24,3072]{1,0:T(8,128)(2,1)}), bf16[768,3072]{1,0:T(8,128)(2,1)}) %all-gather.15.cloned.1.call-update) | async-done | bytes 4718608 | tf_op jit(solution)/shard_map/all_gather | solution.py:207
  275.8 11.5 %multiply_convert_fusion.1 = (bf16[256,3072]{1,0:T(8,128)(2,1)S(1)}, f32[256,3072]{1,0:T(8,128)}, f32[256,3072]{1,0:T(8,128)}) fusion(f32[3072]{0:T(1024)S(1)} %copy-done.48, bf16[768,3072]{1,0:T(8,128)(2,1)} %all-gather.15.cloned.1.call-done, f32[256,768]{1,0:T(8,128)S(1)} %get-tuple-element.609, f32[768]{0:T(1024)S(1)} %copy-done.38, ...), kind=kOutput, calls=%fused_computation.53 | convolution fusion | flops 1260847104 | bytes 13389824 | tf_op jit(solution)/shard_map/dot_general | solution.py:215
  287.3 53.1 %all-gather.17.cloned.1.call-done = bf16[3072,768]{1,0:T(8,128)(2,1)} async-done(((bf16[96,768]{1,0:T(8,128)(2,1)}), bf16[3072,768]{1,0:T(8,128)(2,1)}) %all-gather.17.cloned.1.call-update) | async-done | bytes 4718608 | tf_op jit(solution)/shard_map/all_gather | solution.py:208
  340.5 4.0 fusion.51
  347.5 2.7 convert_reduce_fusion
  350.3 2.3 multiply_reduce_fusion.1
  356.3 13.5 %while.52 = (s32[]{:T(128)}, f32[2,12,128]{2,1,0:T(8,128)S(1)}, s32[2]{0:T(128)S(1)}, s32[2]{0:T(128)S(1)}, bf16[2,1024,768]{1,2,0:T(8,128)(2,1)}, /*index=5*/bf...) while((s32[]{:T(128)}, f32[2,12,128]{2,1,0:T(8,128)S(1)}, ...), condition=%wide.region_16.17_spmd.clone, body=%wide.region_14.16_spmd.clone.sunk | while | flops 408949248 | bytes 22874320 | solution.py:106
  369.8 37.0 %while.53 = (s32[]{:T(128)}, f32[2,128,12,64]{1,3,2,0:T(8,128)}, bf16[2,2,512,12,64]{2,4,3,1,0:T(8,128)(2,1)}, bf16[2,2,512,12,64]{2,4,3,1,0:T(8,128)(2,1)}, s32...) while((s32[]{:T(128)}, f32[2,128,12,64]{1,3,2,0:T(8,128)}, ...), condition=%wide.region_18.19_spmd.clone, body=%wide.region_17.18_spmd.clone.sunk | while | flops 1019610624 | bytes 108679904 | solution.py:140
  374.7 3.9 multiply_convert_fusion.3
  378.6 2.4 bitcast_dynamic-update-slice_fusion.7
  381.0 3.2 fusion.143
  384.3 3.9 bitcast_dynamic-update-slice_fusion.8
  392.9 3.9 multiply_convert_fusion.3
  396.8 2.5 bitcast_dynamic-update-slice_fusion.7
  399.3 3.4 fusion.143
  402.8 3.9 bitcast_dynamic-update-slice_fusion.8
  406.8 5.1 copy.69
  411.9 3.9 convert_element_type.152
  415.8 7.6 copy.74
  426.1 5.1 copy.71
  431.2 3.9 convert_element_type.155
  435.1 7.7 copy.76
  442.8 2.3 copy.86
  448.4 5.2 fusion.44
  455.1 5.1 fusion.55
  462.0 8.3 reduce-scatter.19.cloned.1.call-done
  471.9 47.9 %reduce-scatter.21.cloned.1.call-done = bf16[128,1536]{1,0:T(8,128)(2,1)} async-done(((bf16[1024,1536]{1,0:T(8,128)(2,1)}), bf16[128,1536]{1,0:T(8,128)(2,1)}) %reduce-scatter.21.cloned.1.call-update) | async-done | bytes 393232
  521.5 3.9 convolution_bitcast_fusion.1
  525.5 8.0 copy.78
  534.2 2.3 copy.77
  537.7 41.0 %all-reduce.18 = (f32[768]{0:T(1024)}, f32[768]{0:T(1024)}, f32[768]{0:T(1024)}, f32[768]{0:T(1024)}, f32[768]{0:T(1024)}, /*index=5*/f32[3072]{0:T(1024)}, f32[768]{0:T(1024)}, f32[768]{0:T(1024)}, f32[768]{0:T(1024)S(1)}) all-reduce(f32[768]{0:T(1024)} %reduce_sum.185, ...), channel_id=5, replica_groups=mesh['seq'=8,'slot'=4] {'seq','slot'}, use_global_device_ids=true, to_apply=%region_23.24.clone | all-reduce | flops 9216 | bytes 73728
  589.3 3.4 fusion.30
  592.7 32.7 %reduce-scatter.13.cloned.1.call-done = f32[24,768]{1,0:T(8,128)} async-done(((f32[768,768]{1,0:T(8,128)}), f32[24,768]{1,0:T(8,128)}) %reduce-scatter.13.cloned.1.call-update) | async-done | bytes 73744 | tf_op jit(solution)/shard_map/reduce_scatter | solution.py:309
  625.5 141.6 %reduce-scatter.15.cloned.1.call-done = f32[24,3072]{1,0:T(8,128)} async-done(((f32[768,3072]{1,0:T(8,128)}), f32[24,3072]{1,0:T(8,128)}) %reduce-scatter.15.cloned.1.call-update) | async-done | bytes 294928 | tf_op jit(solution)/shard_map/reduce_scatter | solution.py:317
  767.1 141.6 %reduce-scatter.17.cloned.1.call-done = f32[96,768]{1,0:T(8,128)} async-done(((f32[3072,768]{1,0:T(8,128)}), f32[96,768]{1,0:T(8,128)}) %reduce-scatter.17.cloned.1.call-update) | async-done | bytes 294928 | tf_op jit(solution)/shard_map/reduce_scatter | solution.py:318
  908.7 124.6 %reduce-scatter.23.cloned.1.call-done = f32[24,2304]{1,0:T(8,128)} async-done(((f32[768,2304]{1,0:T(8,128)}), f32[24,2304]{1,0:T(8,128)}) %reduce-scatter.23.cloned.1.call-update) | async-done | bytes 221200
  (331 shorter events, 85.4 us)
Async XLA Ops:
  7.2 66.4 %all-gather.7.cloned.1.call-start = ((), (), s32[]{:S(2)}) async-start(), calls=%async_computation.6 | async-start | bytes 3649536 | tf_op jit(solution)/shard_map/all_gather | solution.py:165
  7.9 124.5 %all-gather.11.cloned.1.call-start = ((), (), s32[]{:S(2)}) async-start(), calls=%async_computation.8 | async-start | bytes 3538944 | tf_op jit(solution)/shard_map/all_gather | solution.py:190
  73.6 4.4 copy-start.51
  73.6 4.7 copy-start.52
  73.6 4.9 copy-start.53
  73.6 5.2 copy-start.54
  73.6 5.4 copy-start.55
  73.6 5.6 copy-start.56
  73.6 5.8 copy-start.57
  73.6 6.1 copy-start.58
  73.6 6.3 copy-start.59
  76.9 45.8 %copy-start.31 = (s32[2]{0:T(128)S(1)}, s32[2]{0:T(128)}, u32[]{:S(2)}) copy-start(s32[2]{0:T(128)} %param.38) | copy-start | bytes 28
  76.9 45.9 %copy-start.30 = (bf16[2,128,768]{2,1,0:T(8,128)(2,1)S(1)}, bf16[2,128,768]{2,1,0:T(8,128)(2,1)}, u32[]{:S(2)}) copy-start(bf16[2,128,768]{2,1,0:T(8,128)(2,1)} %param.39) | copy-start | bytes 1179652
  77.9 76.0 %all-gather.9.cloned.1.call-start = ((), (), s32[]{:S(2)}) async-start(), calls=%async_computation.7 | async-start | bytes 3538944 | tf_op jit(solution)/shard_map/all_gather | solution.py:191
  120.5 90.2 %all-gather.13.cloned.1.call-start = ((), (), s32[]{:S(2)}) async-start(), calls=%async_computation.9 | async-start | bytes 1216512 | tf_op jit(solution)/shard_map/all_gather | solution.py:166
  121.0 154.8 %all-gather.15.cloned.1.call-start = ((), (), s32[]{:S(2)}) async-start(), calls=%async_computation.10 | async-start | bytes 4866048 | tf_op jit(solution)/shard_map/all_gather | solution.py:207
  121.6 218.8 %all-gather.17.cloned.1.call-start = ((), (), s32[]{:S(2)}) async-start(), calls=%async_computation.11 | async-start | bytes 4866048 | tf_op jit(solution)/shard_map/all_gather | solution.py:208
  122.2 348.1 %reduce-scatter.19.cloned.1.call-start = ((), (), s32[]{:S(2)}) async-start(), calls=%async_computation.15 | async-start | bytes 3538944
  171.8 104.0 %copy-start.36 = (f32[768]{0:T(1024)S(1)}, f32[768]{0:T(1024)}, u32[]{:S(2)}) copy-start(f32[768]{0:T(1024)} %convert_element_type.134) | copy-start | bytes 9220
  171.8 104.0 %copy-start.38 = (f32[768]{0:T(1024)S(1)}, f32[768]{0:T(1024)}, u32[]{:S(2)}) copy-start(f32[768]{0:T(1024)} %convert_element_type.135) | copy-start | bytes 9220
  171.8 104.0 %copy-start.48 = (f32[3072]{0:T(1024)S(1)}, f32[3072]{0:T(1024)}, u32[]{:S(2)}) copy-start(f32[3072]{0:T(1024)} %convert_element_type.137) | copy-start | bytes 36868
  173.4 39.4 %copy-start.23 = (bf16[2,128,12,64]{1,0,3,2:T(2,128)(2,1)}, bf16[2,128,12,64]{1,0,3,2:T(2,128)(2,1)S(1)}, u32[]{:S(2)}) copy-start(bf16[2,128,12,64]{1,0,3,2:T(2,128)(2,1)S(1)} %copy.62) | copy-start | bytes 1179652
  212.6 140.0 %copy-start.7 = (f32[256,768]{1,0:T(8,128)}, f32[256,768]{1,0:T(8,128)S(1)}, u32[]{:S(2)}) copy-start(f32[256,768]{1,0:T(8,128)S(1)} %get-tuple-element.609) | copy-start | bytes 2359300
  212.6 140.0 %copy-start.41 = (f32[256]{0:T(256)}, f32[256]{0:T(256)S(1)}, u32[]{:S(2)}) copy-start(f32[256]{0:T(256)S(1)} %broadcast_multiply_fusion.1) | copy-start | bytes 3076
  212.9 139.8 %copy-start.46 = (f32[256]{0:T(256)}, f32[256]{0:T(256)S(1)}, u32[]{:S(2)}) copy-start(f32[256]{0:T(256)S(1)} %fusion.42) | copy-start | bytes 3076
  212.9 127.5 %copy-start.49 = (f32[768]{0:T(1024)S(1)}, f32[768]{0:T(1024)}, u32[]{:S(2)}) copy-start(f32[768]{0:T(1024)} %convert_element_type.139) | copy-start | bytes 9220
  287.3 57.1 %copy-start.15 = (bf16[256,3072]{1,0:T(8,128)(2,1)}, bf16[256,3072]{1,0:T(8,128)(2,1)S(1)}, u32[]{:S(2)}) copy-start(bf16[256,3072]{1,0:T(8,128)(2,1)S(1)} %get-tuple-element.593) | copy-start | bytes 4718596
  340.4 7.1 slice-start.2
  340.4 4.3 copy-start.6
  340.4 4.3 copy-start.40
  340.4 5.2 copy-start.43
  340.4 7.0 slice-start.3
  370.1 4.6 copy-start.34
  374.6 4.0 copy-start
  384.2 3.9 copy-start.35
  384.2 3.9 copy-start.61
  388.2 4.6 copy-start.34
  392.8 4.0 copy-start
  425.8 94.0 %reduce-scatter.21.cloned.1.call-start = ((), (), s32[]{:S(2)}) async-start(), calls=%async_computation.16 | async-start | bytes 3538944
  445.2 180.3 %reduce-scatter.13.cloned.1.call-start = ((), (), s32[]{:S(2)}) async-start(), calls=%async_computation.12 | async-start | bytes 2433024 | tf_op jit(solution)/shard_map/reduce_scatter | solution.py:309
  448.3 318.8 %reduce-scatter.15.cloned.1.call-start = ((), (), s32[]{:S(2)}) async-start(), calls=%async_computation.13 | async-start | bytes 9732096 | tf_op jit(solution)/shard_map/reduce_scatter | solution.py:317
  453.7 455.1 %reduce-scatter.17.cloned.1.call-start = ((), (), s32[]{:S(2)}) async-start(), calls=%async_computation.14 | async-start | bytes 9732096 | tf_op jit(solution)/shard_map/reduce_scatter | solution.py:318
  460.2 573.0 %reduce-scatter.23.cloned.1.call-start = ((), (), s32[]{:S(2)}) async-start(), calls=%async_computation.17 | async-start | bytes 7299072
  461.5 60.0 %copy-start.22 = (bf16[2,128,768]{2,1,0:T(8,128)(2,1)S(1)}, bf16[2,128,768]{2,1,0:T(8,128)(2,1)}, u32[]{:S(2)}) copy-start(bf16[2,128,768]{2,1,0:T(8,128)(2,1)} %param.24) | copy-start | bytes 1179652
  520.9 4.6 copy-start.10
  533.5 4.2 copy-start.44
  533.5 4.2 copy-start.45
  533.5 55.8 %copy-start.9 = (bf16[768,2304]{1,0:T(8,128)(2,1)S(1)}, bf16[768,2304]{1,0:T(8,128)(2,1)}, u32[]{:S(2)}) copy-start(bf16[768,2304]{1,0:T(8,128)(2,1)} %all-gather.7.cloned.1.call-done) | copy-start | bytes 10616836
  (46 other events, 133.6 us)
Sparse Core Ops, SparseCore 0:
  10.8 62.7 all-gather.6
  78.1 31.7 all-gather.10
  120.6 33.3 all-gather.8
  156.6 54.0 all-gather.12
  213.3 62.5 all-gather.14
  278.5 61.8 all-gather.16
  425.9 44.3 reduce-scatter.18
  473.7 46.0 reduce-scatter.20
  525.6 99.7 reduce-scatter.12
  631.8 135.2 reduce-scatter.14
  773.6 135.1 reduce-scatter.16
  914.8 118.4 reduce-scatter.22
where the time goes:
time: 1050 us; the launch traced here: 1040 us
  waiting for transfers between devices  718 us (68%)
  matrix products  97.6 us (9%)
  local copies, waits for them, and re-layouts  96.6 us (9%)
  blocking collectives  80.2 us (8%)
  other arithmetic  25.5 us (2%)
  between operations  15.5 us (1%)
    unnamed x15, waiting for transfers between devices  183 us
    reduce_scatter x1, waiting for transfers between devices, body(): lax.psum_scatter(d_down, ('seq', 'slot'), scatter_dimension=0, tiled=True)  142 us
    reduce_scatter x1, waiting for transfers between devices, body(): lax.psum_scatter(d_up, ('seq', 'slot'), scatter_dimension=0, tiled=True)  142 us
    unnamed x2, blocking collectives  80.2 us
    all_gather x1, waiting for transfers between devices, body(): lax.all_gather(qkv_weight, ('seq', 'slot'), axis=0, tiled=True)  65.6 us
    all_gather x1, waiting for transfers between devices, body(): lax.all_gather(up_weight, ('seq', 'slot'), axis=0, tiled=True)  62.9 us
    all_gather x1, waiting for transfers between devices, body(): lax.all_gather(down_weight, ('seq', 'slot'), axis=0, tiled=True)  53.1 us
    unnamed x147, local copies, waits for them, and re-layouts  50.9 us
  transfers between devices with their start and end apart: 12, of which 11 were waited for; matrix products, arithmetic and copies ran while one was open for 12% of the time, Pallas kernels for 0%

commit v1 on v0

--- a/solution.py
+++ b/solution.py
@@ -6,6 +6,18 @@
 HEADS = 12
 NEG_FILL = -1e30
 EPSILON = 1e-05
+
+
+def collect(shard, axis, dim):
+    ways, here = (lax.axis_size(axis), lax.axis_index(axis))
+    grown, reach = (shard, 1)
+    while reach < ways:
+        theirs = lax.ppermute(grown, axis, [(d, d ^ reach) for d in range(ways)])
+        mine_first = jnp.concatenate([grown, theirs], axis=dim)
+        theirs_first = jnp.concatenate([theirs, grown], axis=dim)
+        grown = jnp.where(here & reach == 0, mine_first, theirs_first)
+        reach = 2 * reach
+    return grown
 
 
 def norm_rows(resid, gain, shift):
@@ -162,7 +174,7 @@
     head_count = HEADS
     flat_rows = tokens.reshape(slot_count * row_count, model_width)
     attn_set = (
-        lax.all_gather(qkv_weight, ("seq", "slot"), axis=0, tiled=True),
+        collect(qkv_weight, ("seq", "slot"), 0),
         lax.all_gather(out_weight, ("seq", "slot"), axis=0, tiled=True),
         lax.all_gather(query_bias, ("seq", "slot"), axis=0, tiled=True),
         lax.all_gather(value_bias, ("seq", "slot"), axis=0, tiled=True),

time: 1050 us -> 1130 us (1.076)
  waiting for transfers between devices: 718 us -> 796 us
    ppermute x0 -> x5, waiting for transfers between devices: none -> 73.3 us  [collect(): theirs = lax.ppermute(grown, axis, [(d, d ^ reach) for d in range(ways)])]
    reduce_scatter x1, waiting for transfers between devices: 32.7 us -> 100 us  [body(): lax.psum_scatter(d_out, ('seq', 'slot'), scatter_dimension=0, tiled=True)]
    all_gather x1, waiting for transfers between devices: 65.6 us -> 1.99 us  [body(): lax.all_gather(qkv_weight, ('seq', 'slot'), axis=0, tiled=True)]
    unnamed x147 -> x153, local copies, waits for them, and re-layouts: 50.9 us -> 44.3 us
  transfers between devices with their start and end apart: 12 -> 17, of which waited for: 11 -> 16; matrix products, arithmetic and copies ran while one was open for 12% -> 11% of each run, Pallas kernels for 0% -> 0%
where the time goes in v1:
time: 1130 us
  waiting for transfers between devices  796 us (70%)
  matrix products  98.1 us (9%)
  local copies, waits for them, and re-layouts  89.3 us (8%)
  blocking collectives  81.7 us (7%)
  other arithmetic  29.7 us (3%)
  between operations  15.6 us (1%)
    unnamed x15, waiting for transfers between devices  183 us
    reduce_scatter x1, waiting for transfers between devices, body(): lax.psum_scatter(d_down, ('seq', 'slot'), scatter_dimension=0, tiled=True)  142 us
    reduce_scatter x1, waiting for transfers between devices, body(): lax.psum_scatter(d_up, ('seq', 'slot'), scatter_dimension=0, tiled=True)  142 us
    reduce_scatter x1, waiting for transfers between devices, body(): lax.psum_scatter(d_out, ('seq', 'slot'), scatter_dimension=0, tiled=True)  100 us
    unnamed x2, blocking collectives  81.7 us
    ppermute x5, waiting for transfers between devices, collect(): theirs = lax.ppermute(grown, axis, [(d, d ^ reach) for d in range(ways)])  73.3 us
    all_gather x1, waiting for transfers between devices, body(): lax.all_gather(up_weight, ('seq', 'slot'), axis=0, tiled=True)  62.9 us
    all_gather x1, waiting for transfers between devices, body(): lax.all_gather(down_weight, ('seq', 'slot'), axis=0, tiled=True)  53 us
  transfers between devices with their start and end apart: 17, of which 16 were waited for; matrix products, arithmetic and copies ran while one was open for 11% of the time, Pallas kernels for 0%

profile of v1, /device:TPU:0, one launch (start us, length us, event | category | flops | bytes accessed | tf_op | source)
XLA Modules:
  0.0 1126.4 jit_solution(16234625292130371162)
XLA Ops:
  7.2 3.1 collective-permute-start
  10.3 3.3 collective-permute-done
  14.6 2.8 collective-permute-start.1
  17.5 9.5 collective-permute-done.1
  30.5 20.3 %collective-permute-done.3 = bf16[192,2304]{1,0:T(8,128)(2,1)S(1)} collective-permute-done((bf16[192,2304]{1,0:T(8,128)(2,1)S(1)}, bf16[192,2304]{1,0:T(8,128)(2,1)S(1)}, u32[]{:S(2)}, u32[]{:S(2)}) %collective-permute-start.3) | collective-permute-done | bytes 884768 | tf_op jit(solution)/shard_map/ppermute | solution.py:15
  52.8 38.5 %collective-permute-done.4 = bf16[384,2304]{1,0:T(8,128)(2,1)} collective-permute-done((bf16[384,2304]{1,0:T(8,128)(2,1)S(1)}, bf16[384,2304]{1,0:T(8,128)(2,1)}, u32[]{:S(2)}, u32[]{:S(2)}) %collective-permute-start.4) | collective-permute-done | bytes 1769504 | tf_op jit(solution)/shard_map/ppermute | solution.py:15
  91.4 3.2 convolution_bitcast_fusion.2
  99.2 40.2 %all-reduce.19 = (bf16[3072]{0:T(1024)(128)(2,1)S(1)}, bf16[768]{0:T(1024)(128)(2,1)S(1)}, bf16[768]{0:T(1024)(128)(2,1)S(1)}, bf16[768]{0:T(1024)(128)(2,1)S(1)...) all-reduce(bf16[3072]{0:T(1024)(128)(2,1)S(1)} %dynamic-update-slic, ...), channel_id=1, replica_groups=mesh['seq'=8,'slot'=4] {'seq','slot'}, use_global_device_ids=true, to_apply=%add.5 | all-reduce | flops 9216 | bytes 36864
  151.2 22.2 %while.50 = (s32[]{:T(128)}, f32[2,12,128]{2,1,0:T(8,128)S(1)}, f32[2,12,128]{2,1,0:T(8,128)S(1)}, s32[2]{0:T(128)S(1)}, s32[2]{0:T(128)}, /*index=5*/bf16[2,102...) while((s32[]{:T(128)}, f32[2,12,128]{2,1,0:T(8,128)S(1)}, ...), condition=%wide.region_3.4_spmd.clone, body=%wide.region_0.3_spmd.clone.sunk | while | flops 209207808 | bytes 17861824 | solution.py:77
  154.7 4.1 bitcast_reduce_fusion.2
  158.8 3.5 fusion.126
  165.8 4.1 bitcast_reduce_fusion.2
  169.9 3.5 fusion.126
  175.6 18.6 %while.51 = (s32[]{:T(128)}, f32[2,128,12,64]{1,3,2,0:T(8,128)}, s32[2]{0:T(128)}, bf16[2,1024,768]{1,2,0:T(8,128)(2,1)}, s32[2]{0:T(128)}, /*index=5*/bf16[2,10...) while((s32[]{:T(128)}, f32[2,128,12,64]{1,3,2,0:T(8,128)}, ...), condition=%wide.region_5.6_spmd.clone, body=%wide.region_4.5_spmd.clone.sunk | while | flops 407766528 | bytes 11421897 | solution.py:97
  180.9 3.8 fusion.131
  190.0 4.2 fusion.131
  195.9 36.0 %all-gather.11.cloned.1.call-done = bf16[768,768]{1,0:T(8,128)(2,1)} async-done(((bf16[24,768]{1,0:T(8,128)(2,1)}), bf16[768,768]{1,0:T(8,128)(2,1)}) %all-gather.11.cloned.1.call-update) | async-done | bytes 1179664 | tf_op jit(solution)/shard_map/all_gather | solution.py:178
  234.2 62.9 %all-gather.13.cloned.1.call-done = bf16[768,3072]{1,0:T(8,128)(2,1)} async-done(((bf16[24,3072]{1,0:T(8,128)(2,1)}), bf16[768,3072]{1,0:T(8,128)(2,1)}) %all-gather.13.cloned.1.call-update) | async-done | bytes 4718608 | tf_op jit(solution)/shard_map/all_gather | solution.py:219
  297.2 11.5 %multiply_convert_fusion.1 = (bf16[256,3072]{1,0:T(8,128)(2,1)S(1)}, f32[256,3072]{1,0:T(8,128)}, f32[256,3072]{1,0:T(8,128)}) fusion(f32[3072]{0:T(1024)S(1)} %copy-done.44, bf16[768,3072]{1,0:T(8,128)(2,1)} %all-gather.13.cloned.1.call-done, f32[256,768]{1,0:T(8,128)S(1)} %get-tuple-element.609, f32[768]{0:T(1024)S(1)} %copy-done.32, ...), kind=kOutput, calls=%fused_computation.61 | convolution fusion | flops 1260847104 | bytes 13389824 | tf_op jit(solution)/shard_map/dot_general | solution.py:227
  308.7 53.0 %all-gather.15.cloned.1.call-done = bf16[3072,768]{1,0:T(8,128)(2,1)} async-done(((bf16[96,768]{1,0:T(8,128)(2,1)}), bf16[3072,768]{1,0:T(8,128)(2,1)}) %all-gather.15.cloned.1.call-update) | async-done | bytes 4718608 | tf_op jit(solution)/shard_map/all_gather | solution.py:220
  361.8 4.0 fusion.58
  368.8 2.7 convert_reduce_fusion
  377.6 14.8 %while.52 = (s32[]{:T(128)}, f32[2,12,128]{2,1,0:T(8,128)S(1)}, s32[2]{0:T(128)S(1)}, s32[2]{0:T(128)}, bf16[2,1024,768]{1,2,0:T(8,128)(2,1)}, /*index=5*/bf16[2...) while((s32[]{:T(128)}, f32[2,12,128]{2,1,0:T(8,128)S(1)}, ...), condition=%wide.region_16.17_spmd.clone, body=%wide.region_14.16_spmd.clone.sunk | while | flops 408949248 | bytes 22874320 | solution.py:118
  392.4 38.2 %while.53 = (s32[]{:T(128)}, f32[2,128,12,64]{1,3,2,0:T(8,128)}, bf16[2,2,512,12,64]{2,4,3,1,0:T(8,128)(2,1)}, bf16[2,2,512,12,64]{2,4,3,1,0:T(8,128)(2,1)}, s32...) while((s32[]{:T(128)}, f32[2,128,12,64]{1,3,2,0:T(8,128)}, ...), condition=%wide.region_18.19_spmd.clone, body=%wide.region_17.18_spmd.clone.sunk | while | flops 1019610624 | bytes 108679776 | solution.py:152
  398.0 3.9 multiply_convert_fusion.3
  404.3 3.2 fusion.148
  407.6 3.9 bitcast_dynamic-update-slice_fusion.8
  416.8 3.9 multiply_convert_fusion.3
  423.2 3.4 fusion.148
  426.7 3.9 bitcast_dynamic-update-slice_fusion.8
  430.7 5.1 copy.69
  435.8 3.9 convert_element_type.152
  439.7 7.6 copy.74
  449.9 5.1 copy.71
  455.1 3.9 convert_element_type.155
  459.0 7.7 copy.76
  472.3 5.2 fusion.51
  479.0 5.1 fusion.61
  485.9 8.3 reduce-scatter.19.cloned.1.call-done
  495.8 47.9 %reduce-scatter.21.cloned.1.call-done = bf16[128,1536]{1,0:T(8,128)(2,1)} async-done(((bf16[1024,1536]{1,0:T(8,128)(2,1)}), bf16[128,1536]{1,0:T(8,128)(2,1)}) %reduce-scatter.21.cloned.1.call-update) | async-done | bytes 393232
  545.4 3.9 convolution_bitcast_fusion.1
  549.3 8.0 copy.78
  558.2 41.5 %all-reduce.18 = (f32[768]{0:T(1024)S(1)}, f32[768]{0:T(1024)S(1)}, f32[768]{0:T(1024)S(1)}, f32[768]{0:T(1024)S(1)}, f32[768]{0:T(1024)S(1)}, /*index=5*/f32[30...) all-reduce(f32[768]{0:T(1024)S(1)} %reduce_sum.185, ...), channel_id=5, replica_groups=mesh['seq'=8,'slot'=4] {'seq','slot'}, use_global_device_ids=true, to_apply=%region_23.24.clone | all-reduce | flops 9216 | bytes 73728
  607.0 3.9 fusion.36
  610.9 100.3 %reduce-scatter.13.cloned.1.call-done = f32[24,768]{1,0:T(8,128)} async-done(((f32[768,768]{1,0:T(8,128)}), f32[24,768]{1,0:T(8,128)}) %reduce-scatter.13.cloned.1.call-update) | async-done | bytes 73744 | tf_op jit(solution)/shard_map/reduce_scatter | solution.py:321
  711.2 141.5 %reduce-scatter.15.cloned.1.call-done = f32[24,3072]{1,0:T(8,128)} async-done(((f32[768,3072]{1,0:T(8,128)}), f32[24,3072]{1,0:T(8,128)}) %reduce-scatter.15.cloned.1.call-update) | async-done | bytes 294928 | tf_op jit(solution)/shard_map/reduce_scatter | solution.py:329
  852.7 141.6 %reduce-scatter.17.cloned.1.call-done = f32[96,768]{1,0:T(8,128)} async-done(((f32[3072,768]{1,0:T(8,128)}), f32[96,768]{1,0:T(8,128)}) %reduce-scatter.17.cloned.1.call-update) | async-done | bytes 294928 | tf_op jit(solution)/shard_map/reduce_scatter | solution.py:330
  994.4 124.6 %reduce-scatter.23.cloned.1.call-done = f32[24,2304]{1,0:T(8,128)} async-done(((f32[768,2304]{1,0:T(8,128)}), f32[24,2304]{1,0:T(8,128)}) %reduce-scatter.23.cloned.1.call-update) | async-done | bytes 221200
  (339 shorter events, 103.1 us)
Async XLA Ops:
  7.2 144.0 %all-gather.9.cloned.1.call-start = ((), (), s32[]{:S(2)}) async-start(), calls=%async_computation.7 | async-start | bytes 3538944 | tf_op jit(solution)/shard_map/all_gather | solution.py:202
  7.2 6.4 collective-permute-start
  14.6 12.3 %collective-permute-start.1 = (bf16[48,2304]{1,0:T(8,128)(2,1)S(1)}, bf16[48,2304]{1,0:T(8,128)(2,1)S(1)}, u32[]{:S(2)}, u32[]{:S(2)}) collective-permute-start(bf16[48,2304]{1,0:T(8,128)(2,1)S(1)} %maximum_select_fusion.5), channel_id=1, source_target_pairs={{0,2},{1,3},{2,0},{3,1},{4,6},{5,7},{6,4},{7,5},{8,10},{9,11},{10,... | collective-permute-start | bytes 663560 | tf_op jit(solution)/shard_map/ppermute | solution.py:15
  27.0 1.9 collective-permute-start.2
  29.0 21.8 %collective-permute-start.3 = (bf16[192,2304]{1,0:T(8,128)(2,1)S(1)}, bf16[192,2304]{1,0:T(8,128)(2,1)S(1)}, u32[]{:S(2)}, u32[]{:S(2)}) collective-permute-start(bf16[192,2304]{1,0:T(8,128)(2,1)S(1)} %maximum_select_fusion.3), channel_id=1, source_target_pairs={{0,8},{1,9},{2,10},{3,11},{4,12},{5,13},{6,14},{7,15},{8,0},{9,1},... | collective-permute-start | bytes 2654216 | tf_op jit(solution)/shard_map/ppermute | solution.py:15
  51.3 40.0 %collective-permute-start.4 = (bf16[384,2304]{1,0:T(8,128)(2,1)S(1)}, bf16[384,2304]{1,0:T(8,128)(2,1)}, u32[]{:S(2)}, u32[]{:S(2)}) collective-permute-start(bf16[384,2304]{1,0:T(8,128)(2,1)S(1)} %maximum_select_fusion.2), channel_id=1, source_target_pairs={{0,16},{1,17},{2,18},{3,19},{4,20},{5,21},{6,22},{7,23},{8,24},{9,... | collective-permute-start | bytes 5308424 | tf_op jit(solution)/shard_map/ppermute | solution.py:15
  91.3 5.7 copy-start.51
  91.3 6.0 copy-start.52
  91.3 6.2 copy-start.53
  91.3 6.5 copy-start.54
  91.3 6.7 copy-start.55
  91.3 6.9 copy-start.56
  91.3 7.1 copy-start.57
  91.3 7.4 copy-start.58
  91.3 7.6 copy-start.59
  96.0 49.1 %copy-start.29 = (bf16[2,128,768]{2,1,0:T(8,128)(2,1)S(1)}, bf16[2,128,768]{2,1,0:T(8,128)(2,1)}, u32[]{:S(2)}) copy-start(bf16[2,128,768]{2,1,0:T(8,128)(2,1)} %param.39) | copy-start | bytes 1179652
  97.0 78.2 %all-gather.7.cloned.1.call-start = ((), (), s32[]{:S(2)}) async-start(), calls=%async_computation.6 | async-start | bytes 3538944 | tf_op jit(solution)/shard_map/all_gather | solution.py:203
  141.8 90.2 %all-gather.11.cloned.1.call-start = ((), (), s32[]{:S(2)}) async-start(), calls=%async_computation.8 | async-start | bytes 1216512 | tf_op jit(solution)/shard_map/all_gather | solution.py:178
  142.5 154.6 %all-gather.13.cloned.1.call-start = ((), (), s32[]{:S(2)}) async-start(), calls=%async_computation.9 | async-start | bytes 4866048 | tf_op jit(solution)/shard_map/all_gather | solution.py:219
  143.1 218.6 %all-gather.15.cloned.1.call-start = ((), (), s32[]{:S(2)}) async-start(), calls=%async_computation.10 | async-start | bytes 4866048 | tf_op jit(solution)/shard_map/all_gather | solution.py:220
  143.7 350.5 %reduce-scatter.19.cloned.1.call-start = ((), (), s32[]{:S(2)}) async-start(), calls=%async_computation.15 | async-start | bytes 3538944
  194.3 102.9 %copy-start.30 = (f32[768]{0:T(1024)S(1)}, f32[768]{0:T(1024)}, u32[]{:S(2)}) copy-start(f32[768]{0:T(1024)} %convert_element_type.134) | copy-start | bytes 9220
  194.3 102.9 %copy-start.32 = (f32[768]{0:T(1024)S(1)}, f32[768]{0:T(1024)}, u32[]{:S(2)}) copy-start(f32[768]{0:T(1024)} %convert_element_type.135) | copy-start | bytes 9220
  194.3 102.9 %copy-start.44 = (f32[3072]{0:T(1024)S(1)}, f32[3072]{0:T(1024)}, u32[]{:S(2)}) copy-start(f32[3072]{0:T(1024)} %convert_element_type.137) | copy-start | bytes 36868
  195.9 38.3 %copy-start.21 = (bf16[2,128,12,64]{1,0,3,2:T(2,128)(2,1)}, bf16[2,128,12,64]{1,0,3,2:T(2,128)(2,1)S(1)}, u32[]{:S(2)}) copy-start(bf16[2,128,12,64]{1,0,3,2:T(2,128)(2,1)S(1)} %copy.62) | copy-start | bytes 1179652
  233.9 140.0 %copy-start.7 = (f32[256,768]{1,0:T(8,128)}, f32[256,768]{1,0:T(8,128)S(1)}, u32[]{:S(2)}) copy-start(f32[256,768]{1,0:T(8,128)S(1)} %get-tuple-element.609) | copy-start | bytes 2359300
  233.9 140.0 %copy-start.35 = (f32[256]{0:T(256)}, f32[256]{0:T(256)S(1)}, u32[]{:S(2)}) copy-start(f32[256]{0:T(256)S(1)} %broadcast_multiply_fusion.1) | copy-start | bytes 3076
  234.2 139.8 %copy-start.42 = (f32[256]{0:T(256)}, f32[256]{0:T(256)S(1)}, u32[]{:S(2)}) copy-start(f32[256]{0:T(256)S(1)} %fusion.48) | copy-start | bytes 3076
  234.2 127.5 %copy-start.46 = (f32[768]{0:T(1024)S(1)}, f32[768]{0:T(1024)}, u32[]{:S(2)}) copy-start(f32[768]{0:T(1024)} %convert_element_type.139) | copy-start | bytes 9220
  308.7 57.1 %copy-start.13 = (bf16[256,3072]{1,0:T(8,128)(2,1)}, bf16[256,3072]{1,0:T(8,128)(2,1)S(1)}, u32[]{:S(2)}) copy-start(bf16[256,3072]{1,0:T(8,128)(2,1)S(1)} %get-tuple-element.593) | copy-start | bytes 4718596
  361.7 7.1 slice-start.2
  361.7 4.3 copy-start.6
  361.7 4.3 copy-start.34
  361.7 5.2 copy-start.37
  361.8 7.0 slice-start.3
  397.3 4.6 copy-start
  407.6 3.9 copy-start.17
  407.6 3.9 copy-start.61
  416.1 4.6 copy-start
  449.6 94.0 %reduce-scatter.21.cloned.1.call-start = ((), (), s32[]{:S(2)}) async-start(), calls=%async_computation.16 | async-start | bytes 3538944
  469.0 137.9 %all-gather.17.cloned.1.call-start = ((), (), s32[]{:S(2)}) async-start(), calls=%async_computation.11 | async-start | bytes 3649536 | tf_op jit(solution)/shard_map/all_gather | solution.py:238
  469.8 241.4 %reduce-scatter.13.cloned.1.call-start = ((), (), s32[]{:S(2)}) async-start(), calls=%async_computation.12 | async-start | bytes 2433024 | tf_op jit(solution)/shard_map/reduce_scatter | solution.py:321
  472.2 380.6 %reduce-scatter.15.cloned.1.call-start = ((), (), s32[]{:S(2)}) async-start(), calls=%async_computation.13 | async-start | bytes 9732096 | tf_op jit(solution)/shard_map/reduce_scatter | solution.py:329
  477.6 516.8 %reduce-scatter.17.cloned.1.call-start = ((), (), s32[]{:S(2)}) async-start(), calls=%async_computation.14 | async-start | bytes 9732096 | tf_op jit(solution)/shard_map/reduce_scatter | solution.py:330
  484.1 634.9 %reduce-scatter.23.cloned.1.call-start = ((), (), s32[]{:S(2)}) async-start(), calls=%async_computation.17 | async-start | bytes 7299072
  485.4 60.0 %copy-start.28 = (bf16[2,128,768]{2,1,0:T(8,128)(2,1)S(1)}, bf16[2,128,768]{2,1,0:T(8,128)(2,1)}, u32[]{:S(2)}) copy-start(bf16[2,128,768]{2,1,0:T(8,128)(2,1)} %param.24) | copy-start | bytes 1179652
  557.4 49.6 %copy-start.12 = (f32[256,768]{1,0:T(8,128)S(1)}, f32[256,768]{1,0:T(8,128)}, u32[]{:S(2)}) copy-start(f32[256,768]{1,0:T(8,128)} %copy-done.11) | copy-start | bytes 2359300
  557.4 49.6 %copy-start.50 = (f32[256]{0:T(256)S(1)}, f32[256]{0:T(256)}, u32[]{:S(2)}) copy-start(f32[256]{0:T(256)} %copy-done.49) | copy-start | bytes 3076
  (48 other events, 121.8 us)
Sparse Core Ops, SparseCore 0:
  97.1 33.9 all-gather.8
  141.9 33.1 all-gather.6
  177.9 53.9 all-gather.10
  234.6 62.5 all-gather.12
  299.8 61.8 all-gather.14
  449.8 44.3 reduce-scatter.18
  497.6 46.0 reduce-scatter.20
  546.5 60.4 all-gather.16
  612.8 98.3 reduce-scatter.12
  717.5 135.1 reduce-scatter.14
  859.2 135.0 reduce-scatter.16
  1000.5 118.4 reduce-scatter.22
